TPU v7x, 512 devices: a whole 4x4x16 slice. The times are simulated.
512 devices in a mesh: head: 8 (over x, core), ctx: 64 (over y, z).
Axes of the slice: x: 4, y: 4, z: 16, core: 2. Of those that a mesh axis runs over, the one named last changes fastest.
Arguments:
- queries: bfloat16 [32768, 4096], P('ctx', 'head'), may hold values from -26.25 to 26.25
- keys: bfloat16 [32768, 1024], P(('ctx', 'head')), may hold values from -7.5 to 7.5
- values: bfloat16 [32768, 1024], P(('ctx', 'head')), may hold values from -5 to 5
- selected: int32 [8, 64, 3], P('head'), may hold values from 0 to 63, as said below
Outputs:
- attended: bfloat16 [32768, 4096], P('ctx', 'head')
Inputs may be any that keep to these rules, and one draw needn't show every extreme that they name: `selected`: row b of every key-value head holds b in slot 0; its other 2 slots hold distinct blocks below b, or b again where fewer than 2 blocks lie below b.
All inputs are finite; a program needn't handle non-finite values.
Results may differ from a plain program's by a relative error of at most 0.0041.
Values may be sent and summed in bfloat16 or wider, within the bound.
A program may use at most 64 MiB of HBM per device.

v0:
```python
import jax
import jax.numpy as jnp
from jax import lax
from jax.sharding import PartitionSpec as P

HD = 128
QH = 4
BLK = 512


def attend_block(inputs):
    query_block, own_keys, own_values, tile_keys, tile_values, slot_live = inputs
    block_len = own_keys.shape[0]
    head_size = own_keys.shape[1]
    factor = head_size ** (-0.5)
    key_rows = jnp.concatenate([own_keys[None], tile_keys], axis=0).reshape(-1, head_size)
    value_rows = jnp.concatenate([own_values[None], tile_values], axis=0).reshape(-1, head_size)
    positions = jnp.arange(block_len, dtype=jnp.int32)
    causal = positions[:, None] >= positions[None, :]
    others = jnp.broadcast_to(slot_live[None, :, None], (block_len, slot_live.shape[0], block_len))
    allowed = jnp.concatenate([causal[:, None, :], others], axis=1).reshape(block_len, -1)

    def per_head(query_head):
        scores = (
            jnp.einsum("qd,kd->qk", query_head, key_rows, preferred_element_type=jnp.float32)
            * factor
        )
        scores = jnp.where(allowed, scores, -jnp.inf)
        top_score = jnp.max(scores, axis=1, keepdims=True)
        weights = jnp.exp(scores - top_score)
        weight_sum = jnp.sum(weights, axis=1)
        product = jnp.dot(
            weights.astype(jnp.bfloat16), value_rows, preferred_element_type=jnp.float32
        )
        return (product / weight_sum[:, None]).astype(jnp.bfloat16)

    return lax.map(per_head, query_block)


def on_device(queries, keys, values, selected):
    key_local, value_local = (
        lax.all_to_all(keys, "head", split_axis=1, concat_axis=0, tiled=True),
        lax.all_to_all(values, "head", split_axis=1, concat_axis=0, tiled=True),
    )
    rows_here = key_local.shape[0]
    query_blocks = rows_here // BLK
    ctx_rank = lax.axis_index("ctx")
    first_block = ctx_rank * query_blocks
    chosen = selected[0]
    own_lists = lax.dynamic_slice_in_dim(chosen, first_block, query_blocks, 0)
    query_heads = queries.reshape(query_blocks, BLK, QH, HD).transpose(0, 2, 1, 3)
    own_keys = key_local.reshape(query_blocks, BLK, HD)
    own_values = value_local.reshape(query_blocks, BLK, HD)
    full_keys, full_values = (
        lax.all_gather(key_local, "ctx", axis=0, tiled=True),
        lax.all_gather(value_local, "ctx", axis=0, tiled=True),
    )
    full_keys = full_keys.reshape(-1, BLK, HD)
    full_values = full_values.reshape(-1, BLK, HD)
    tile_keys = full_keys[own_lists[:, 1:]]
    tile_values = full_values[own_lists[:, 1:]]
    block_ids = first_block + jnp.arange(query_blocks, dtype=jnp.int32)
    slot_live = own_lists[:, 1:] != block_ids[:, None]
    stacked = lax.map(
        attend_block, (query_heads, own_keys, own_values, tile_keys, tile_values, slot_live)
    )
    return stacked.transpose(0, 2, 1, 3).reshape(rows_here, QH * HD)


def solution(mesh):
    return jax.shard_map(
        on_device,
        mesh=mesh,
        in_specs=(
            P("ctx", "head"),
            P(("ctx", "head"), None),
            P(("ctx", "head"), None),
            P("head", None, None),
        ),
        out_specs=P("ctx", "head"),
        check_vma=False,
    )
```

profile of v0, /device:TPU:24, one launch (start us, length us, event | category | flops | bytes accessed | tf_op | source)
XLA Modules:
  0.0 350.8 jit_solution(1623748749131682620)
XLA Ops:
  6.5 0.0 copy-start
  6.5 0.0 copy-start.3
  6.5 0.0 all-gather.3.cloned.1.call-start
  6.5 0.9 copy-done
  7.5 10.3 %all_to_all.38 = bf16[64,8,128]{2,0,1:T(8,128)(2,1)} all-to-all(bf16[64,8,128]{2,0,1:T(8,128)(2,1)S(1)} %copy_bitcast_fusion.2), channel_id=1, replica_groups=mesh['head'=8,'ctx'=64] {'head'}, dimensions={1} | all-to-all | bytes 262144 | tf_op jit(solution)/shard_map/all_to_all | solution.py:42
  17.8 0.0 copy-start.1
  17.8 0.0 all-gather.3.cloned.1.call-update
  17.8 0.0 all-gather.5.cloned.1.call-start
  17.9 0.9 copy_bitcast_fusion.1
  18.8 9.2 %all_to_all.39 = bf16[64,8,128]{2,0,1:T(8,128)(2,1)} all-to-all(bf16[64,8,128]{2,0,1:T(8,128)(2,1)S(1)} %copy_bitcast_fusion.1), channel_id=1, replica_groups=mesh['head'=8,'ctx'=64] {'head'}, dimensions={1} | all-to-all | bytes 262144 | tf_op jit(solution)/shard_map/all_to_all | solution.py:43
  28.0 0.0 copy-start.2
  28.0 0.0 all-gather.5.cloned.1.call-update
  28.0 0.9 dynamic-slice_reduce_fusion
  29.0 0.1 compare_bitcast_fusion
  29.1 0.1 pad.3.clone
  29.1 0.1 iota_compare_fusion
  29.2 0.3 pad_add_fusion
  29.6 0.9 copy.30
  30.5 0.0 copy-done.3
  30.5 0.2 copy.26
  30.7 0.1 fusion.21
  30.8 144.5 %all-gather.3.cloned.1.call-done = bf16[32768,128]{1,0:T(8,128)(2,1)} async-done(((bf16[512,128]{1,0:T(8,128)(2,1)}), bf16[32768,128]{1,0:T(8,128)(2,1)}) %all-gather.3.cloned.1.call-update) | async-done | bytes 8388624 | tf_op jit(solution)/shard_map/all_gather | solution.py:55
  175.3 4.0 %gather_fusion = bf16[2,512,128]{2,1,0:T(8,128)(2,1)S(1)} fusion(bf16[64,512,128]{2,1,0:T(8,128)(2,1)} %bitcast.73, s32[1024]{0:T(1024)S(1)} %pad_clamp_fusion), kind=kCustom, calls=%fused_computation | custom fusion | bytes 524296 | tf_op jit(solution)/shard_map/gather | solution.py:60
  179.3 150.8 %all-gather.5.cloned.1.call-done = bf16[32768,128]{1,0:T(8,128)(2,1)} async-done(((bf16[512,128]{1,0:T(8,128)(2,1)}), bf16[32768,128]{1,0:T(8,128)(2,1)}) %all-gather.5.cloned.1.call-update) | async-done | bytes 8388624 | tf_op jit(solution)/shard_map/all_gather | solution.py:56
  330.0 4.0 %gather_fusion.1 = bf16[2,512,128]{2,1,0:T(8,128)(2,1)S(1)} fusion(bf16[64,512,128]{2,1,0:T(8,128)(2,1)} %bitcast.74, s32[1024]{0:T(1024)S(1)} %pad_clamp_fusion), kind=kCustom, calls=%fused_computation.1 | custom fusion | bytes 524296 | tf_op jit(solution)/shard_map/gather | solution.py:61
  334.0 0.0 copy-done.1
  334.1 0.0 copy-done.2
  334.1 8.5 %while.17 = (s32[]{:T(128)}, bf16[4,512,128]{2,1,0:T(8,128)(2,1)S(1)}, bf16[4,512,128]{1,2,0:T(8,128)(2,1)S(1)}, bf16[1536,128]{1,0:T(8,128)(2,1)S(1)}, pred[512...) while((s32[]{:T(128)}, bf16[4,512,128]{2,1,0:T(8,128)(2,1)S(1)}, ...), condition=%wide.region_3.4_spmd, body=%wide.region_0.3_spmd.sunk | while | flops 408288256 | bytes 11282525 | solution.py:37
  334.2 0.8 fusion.36
  335.0 0.6 fusion.37
  335.6 0.7 fusion.38
  336.3 0.8 fusion.36
  337.1 0.6 fusion.37
  337.7 0.7 fusion.38
  338.4 0.8 fusion.36
  339.2 0.6 fusion.37
  339.8 0.7 fusion.38
  340.5 0.8 fusion.36
  341.3 0.6 fusion.37
  341.9 0.7 fusion.38
  342.6 0.4 copy.31
  343.0 0.9 copy.39
  (5 shorter events, 0.1 us)
Async XLA Ops:
  6.5 0.9 copy-start
  6.5 23.9 %copy-start.3 = (bf16[512,512]{1,0:T(8,128)(2,1)S(1)}, bf16[512,512]{1,0:T(8,128)(2,1)}, u32[]{:S(2)}) copy-start(bf16[512,512]{1,0:T(8,128)(2,1)} %param.6) | copy-start | bytes 1572868
  6.5 168.7 %all-gather.3.cloned.1.call-start = ((), (), s32[]{:S(2)}) async-start(), calls=%async_computation.2 | async-start | bytes 8519680 | tf_op jit(solution)/shard_map/all_gather | solution.py:55
  17.8 316.2 %copy-start.1 = (bf16[64,8,128]{2,0,1:T(8,128)(2,1)S(1)}, bf16[64,8,128]{2,0,1:T(8,128)(2,1)}, u32[]{:S(2)}) copy-start(bf16[64,8,128]{2,0,1:T(8,128)(2,1)} %all_to_all.38) | copy-start | bytes 393220
  17.8 312.2 %all-gather.5.cloned.1.call-start = ((), (), s32[]{:S(2)}) async-start(), calls=%async_computation.3 | async-start | bytes 8519680 | tf_op jit(solution)/shard_map/all_gather | solution.py:56
  28.0 306.1 %copy-start.2 = (bf16[64,8,128]{2,0,1:T(8,128)(2,1)S(1)}, bf16[64,8,128]{2,0,1:T(8,128)(2,1)}, u32[]{:S(2)}) copy-start(bf16[64,8,128]{2,0,1:T(8,128)(2,1)} %all_to_all.39) | copy-start | bytes 393220
Sparse Core Ops, SparseCore 0:
  18.0 157.2 all-gather.2
  178.2 151.7 all-gather.4
where the time goes:
time: 353 us; the launch traced here: 351 us
  waiting for transfers between devices  295 us (84%)
  blocking collectives  19.5 us (6%)
  between operations  13.5 us (4%)
  local copies, waits for them, and re-layouts  13.2 us (4%)
  matrix products  6.1 us (2%)
    all_gather x1, waiting for transfers between devices, on_device(): lax.all_gather(value_local, 'ctx', axis=0, tiled=True)  151 us
    all_gather x1, waiting for transfers between devices, on_device(): lax.all_gather(key_local, 'ctx', axis=0, tiled=True)  144 us
    all_to_all x1, blocking collectives, on_device(): lax.all_to_all(keys, 'head', split_axis=1, concat_axis=0, tiled=True)  10.3 us
    all_to_all x1, blocking collectives, on_device(): lax.all_to_all(values, 'head', split_axis=1, concat_axis=0, tiled=True)  9.19 us
  transfers between devices with their start and end apart: 2, of which 2 were waited for; matrix products, arithmetic and copies ran while one was open for 2% of the time, Pallas kernels for 0%

commit v1 on v0

v1 whole, which is shorter than its diff:
```python
import functools

import jax
import jax.numpy as jnp
from jax import lax
from jax.experimental import pallas as pl
from jax.experimental.pallas import tpu as pltpu
from jax.sharding import PartitionSpec as P

MESH = pl.DeviceIdType.MESH
HD = 128
QH = 4
BLK = 512
KVH = 8
NB = 64
NY = 4
NZ = 16
PIECE = 16
SLICE = BLK // KVH
ROWS = 128
LOG2E = 1.4426950408889634
SCALE = HD ** (-0.5) * LOG2E


def partner(me, t):
    k = NZ - 1 - t // NY
    dy = t % NY
    dz = ((k + 1) // 2) * (2 * (k % 2) - 1)
    return ((me // NZ + dy) % NY) * NZ + (me % NZ + dz + NZ) % NZ


def keeper(head, q):
    return ((head // 2 + q) % NY) * NZ + 2 * q + head % 2


def kept(me):
    y, z = me // NZ, me % NZ
    q = z // 2
    head = ((y + 2 * NY - q) % NY) * 2 + z % 2
    return (q // 4) * 32 + head * 4 + q % 4


def scores(q, k):
    return lax.dot_general(q, k, (((1,), (1,)), ((), ())), preferred_element_type=jnp.float32)


def weighted(p, v):
    ones = jnp.ones_like(v)
    return jnp.dot(p.astype(jnp.bfloat16), jnp.concatenate([v, ones], axis=1), preferred_element_type=jnp.float32)


def kernel(
    queries, keys, values, selected, out,
    q_ref, sel, own, pieces, picked, fetched, top, acc, o_ref,
    q_sem, sel_sem, head_send, head_recv, spread_send, spread_recv, fetch_send, fetch_recv, out_sem,
):
    me = lax.axis_index("ctx")
    head = lax.axis_index("head")
    x, core = head // 2, head % 2

    barrier = pltpu.get_barrier_semaphore()

    def greet(t, carry):
        pl.semaphore_signal(barrier, inc=1, device_id={"ctx": (me + t + 1) % NB}, device_id_type=MESH)
        return carry

    lax.fori_loop(0, NB - 1, greet, 0)
    for j in range(1, KVH):
        pl.semaphore_signal(barrier, inc=1, device_id={"head": (head + j) % KVH}, device_id_type=MESH)

    q_copy = pltpu.make_async_copy(queries, q_ref, q_sem)
    q_copy.start()
    sel_copy = pltpu.make_async_copy(selected, sel, sel_sem)
    sel_copy.start()
    for kv, source in enumerate((keys, values)):
        columns = pl.ds(pl.multiple_of(head * HD, HD), HD)
        pltpu.make_async_copy(source.at[:, columns], own.at[kv, head], head_recv.at[head]).start()
    sel_copy.wait()

    pl.semaphore_wait(barrier, NB - 1 + KVH - 1)

    order = [(dx, dk) for dx in (0, 1, 3, 2) for dk in (0, 1)]
    for dx, dk in order[1:]:
        g = ((x + dx) % 4) * 2 + (core + dk) % 2
        for kv, source in enumerate((keys, values)):
            columns = pl.ds(pl.multiple_of(g * HD, HD), HD)
            pltpu.make_async_remote_copy(
                src_ref=source.at[:, columns], dst_ref=own.at[kv, head], send_sem=head_send,
                recv_sem=head_recv.at[head], device_id={"head": g}, device_id_type=MESH,
            ).start()

    for dx, dk in order:
        g = ((x + (4 - dx)) % 4) * 2 + (core + dk) % 2
        pltpu.make_async_copy(own.at[:, g], own.at[:, g], head_recv.at[g]).wait()
        for q in range(8):
            to = keeper(g, q)
            source = own.at[q // 4, g, pl.ds(PIECE * (q % 4), PIECE)]

            @pl.when(to != me)
            def _():
                pltpu.make_async_remote_copy(
                    src_ref=source, dst_ref=pieces.at[me], send_sem=spread_send,
                    recv_sem=spread_recv, device_id={"ctx": to}, device_id_type=MESH,
                ).start()

            @pl.when(to == me)
            def _():
                pltpu.make_async_copy(source, pieces.at[me], spread_recv).start()

    pltpu.make_async_copy(pieces, pieces, spread_recv).wait()

    def pick(d, carry):
        picked[d, 0] = pieces[sel[0, d, 1]]
        picked[d, 1] = pieces[sel[0, d, 2]]
        return carry

    lax.fori_loop(0, NB, pick, 0)
    mine = kept(me)

    def send(t, carry):
        d = partner(me, t)

        @pl.when(d != me)
        def _():
            pltpu.make_async_remote_copy(
                src_ref=picked.at[d], dst_ref=fetched.at[mine], send_sem=fetch_send,
                recv_sem=fetch_recv, device_id={"ctx": d}, device_id_type=MESH,
            ).start()

        @pl.when(d == me)
        def _():
            pltpu.make_async_copy(picked.at[d], fetched.at[mine], fetch_recv).start()

        return carry

    lax.fori_loop(0, NB, send, 0)

    q_copy.wait()

    def own_block(h, carry):
        columns = pl.ds(pl.multiple_of(h * HD, HD), HD)
        for r in range(BLK // ROWS):
            rows, width = pl.ds(r * ROWS, ROWS), (r + 1) * ROWS
            k = own[0].reshape(BLK, HD)[:width]
            v = own[1].reshape(BLK, HD)[:width]
            s = scores(q_ref[rows, columns], k)
            at = lax.broadcasted_iota(jnp.int32, s.shape, 0) + r * ROWS
            s = jnp.where(lax.broadcasted_iota(jnp.int32, s.shape, 1) <= at, s, -jnp.inf)
            m = jnp.max(s, axis=1, keepdims=True)
            acc[h, rows] = weighted(jnp.exp2((s - m) * SCALE), v)
            top[h, rows] = jnp.broadcast_to(m, (ROWS, HD))
        return carry

    lax.fori_loop(0, QH, own_block, 0)

    pltpu.make_async_copy(fetched, fetched, fetch_recv).wait()
    gone = [jnp.where(sel[0, me, s + 1] != me, 0.0, jnp.inf).astype(jnp.float32) for s in range(2)]

    def others(i, carry):
        h, r = i // (BLK // ROWS), i % (BLK // ROWS)
        columns = pl.ds(pl.multiple_of(h * HD, HD), HD)
        rows = pl.ds(pl.multiple_of(r * ROWS, ROWS), ROWS)
        q = q_ref[rows, columns]
        m0 = top[h, rows][:, :1]
        m = m0
        parts = []
        for s in range(2):
            part = scores(q, fetched[:32, s].reshape(BLK, HD))
            m = jnp.maximum(m, jnp.max(part, axis=1, keepdims=True) - gone[s])
            parts.append(part)
        total = acc[h, rows] * jnp.exp2((m0 - m) * SCALE)
        for s in range(2):
            p = jnp.exp2((parts[s] - (m + gone[s])) * SCALE)
            total += weighted(p, fetched[32:, s].reshape(BLK, HD))
        o_ref[rows, columns] = (total[:, :HD] / total[:, HD:]).astype(o_ref.dtype)
        return carry

    lax.fori_loop(0, QH * BLK // ROWS, others, 0)
    out_copy = pltpu.make_async_copy(o_ref, out, out_sem)
    out_copy.start()

    most = pl.ds(0, KVH - 1)
    pltpu.make_async_copy(own.at[:, most], own.at[:, most], head_send).wait()
    most = pl.ds(0, NB - 1)
    pltpu.make_async_copy(pieces.at[most], pieces.at[most], spread_send).wait()
    pltpu.make_async_copy(picked.at[most], picked.at[most], fetch_send).wait()
    out_copy.wait()


def on_device(queries, keys, values, selected):
    dma = pltpu.SemaphoreType.DMA
    hbm = pl.BlockSpec(memory_space=pl.ANY)
    return pl.pallas_call(
        kernel,
        out_shape=jax.ShapeDtypeStruct((BLK, QH * HD), jnp.bfloat16),
        in_specs=[hbm, hbm, hbm, hbm],
        out_specs=hbm,
        scratch_shapes=[
            pltpu.VMEM((BLK, QH * HD), jnp.bfloat16),
            pltpu.SMEM((1, NB, 3), jnp.int32),
            pltpu.VMEM((2, KVH, SLICE, HD), jnp.bfloat16),
            pltpu.VMEM((NB, PIECE, HD), jnp.bfloat16),
            pltpu.VMEM((NB, 2, PIECE, HD), jnp.bfloat16),
            pltpu.VMEM((NB, 2, PIECE, HD), jnp.bfloat16),
            pltpu.VMEM((QH, BLK, HD), jnp.float32),
            pltpu.VMEM((QH, BLK, 2 * HD), jnp.float32),
            pltpu.VMEM((BLK, QH * HD), jnp.bfloat16),
            dma, dma, dma, dma((KVH,)), dma, dma, dma, dma, dma,
        ],
        compiler_params=pltpu.CompilerParams(collective_id=0, has_side_effects=True),
    )(queries, keys, values, selected)


def solution(mesh):
    return jax.shard_map(
        on_device,
        mesh=mesh,
        in_specs=(
            P("ctx", "head"),
            P(("ctx", "head"), None),
            P(("ctx", "head"), None),
            P("head", None, None),
        ),
        out_specs=P("ctx", "head"),
        check_vma=False,
    )
```

time: 353 us -> 73.5 us (0.21)
  waiting for transfers between devices: 295 us -> 0 us
  Pallas kernels: 0 us -> 68.9 us
  blocking collectives: 19.5 us -> 0 us
  between operations: 13.5 us -> 0.01 us
  local copies, waits for them, and re-layouts: 13.2 us -> 3.25 us
  matrix products: 6.1 us -> 0 us
    all_gather x2 -> x0, waiting for transfers between devices: 295 us -> none  [the longest x1 151 us: on_device(): lax.all_gather(value_local, 'ctx', axis=0, tiled=True)]
    pallas_call x0 -> x1, Pallas kernels: none -> 68.9 us  [on_device(): pl.pallas_call(kernel, out_shape=jax.ShapeDtypeStruct((BLK, QH * HD), jnp...]
    all_to_all x2 -> x0, blocking collectives: 19.5 us -> none  [the longest x1 10.3 us: on_device(): lax.all_to_all(keys, 'head', split_axis=1, concat_axis=0, tiled=True)]
    gather x2 -> x0, local copies, waits for them, and re-layouts: 7.95 us -> none  [the longest x1 3.98 us: on_device(): tile_keys = full_keys[own_lists[:, 1:]]]
    dot_general x8 -> x0, matrix products: 6.1 us -> none  [the longest x4 3.27 us: per_head(): jnp.einsum('qd,kd->qk', query_head, key_rows, preferred_element_type=jnp....]
  transfers between devices with their start and end apart: 2 -> 0, of which waited for: 2 -> 0; matrix products, arithmetic and copies ran while one was open for 2% -> 0% of each run, Pallas kernels for 0% -> 0%
where the time goes in v1:
time: 73.5 us; the launch traced here: 72.2 us
  Pallas kernels  68.9 us (94%)
  local copies, waits for them, and re-layouts  3.25 us (4%)
    pallas_call x1, Pallas kernels, on_device(): pl.pallas_call(kernel, out_shape=jax.ShapeDtypeStruct((BLK, QH * HD), jnp...  68.9 us
    unnamed x2, local copies, waits for them, and re-layouts  3.25 us

profile of v1, /device:TPU:24, one launch (start us, length us, event | category | flops | bytes accessed | tf_op | source)
XLA Modules:
  0.0 72.2 jit_solution(12042939473758999410)
XLA Ops:
  0.0 1.4 %copy.5.selected = s32[1,64,3]{2,1,0:T(8,128)} copy(s32[1,64,3]{1,0,2:T(1,128)} %param.7) | data formatting | bytes 1536 | tf_op args[3]
  1.4 68.9 %shard_map.46 = bf16[512,512]{1,0:T(8,128)(2,1)} custom-call(bf16[512,512]{1,0:T(8,128)(2,1)} %queries.1, bf16[64,1024]{1,0:T(8,128)(2,1)} %keys.1, bf16[64,1024]{1,0:T(8,128)(2,1)} %values.1, s32[1,64,3]{2,1,0:T(8,128)} %copy.5.selected), custom_call_target="tpu_custom_call" | custom-call | tf_op jit(solution)/shard_map/pallas_call | solution.py:193
  70.3 1.9 %copy.7 = bf16[512,512]{1,0:T(8,128)(2,1)} copy(bf16[512,512]{1,0:T(8,128)(2,1)} %shard_map.46) | data formatting | bytes 1048576

commit v2 on v1

v2 whole, which is shorter than its diff:
```python
import functools

import jax
import jax.numpy as jnp
from jax import lax
from jax.experimental import pallas as pl
from jax.experimental.pallas import tpu as pltpu
from jax.sharding import PartitionSpec as P

MESH = pl.DeviceIdType.MESH
HD = 128
QH = 4
BLK = 512
KVH = 8
NB = 64
NY = 4
NZ = 16
GROUPS = 4
PIECE = 16
SLICE = BLK // KVH
ROWS = 128
LOG2E = 1.4426950408889634
SCALE = HD ** (-0.5) * LOG2E


STEPS = [8, 9, 7, 10, 6, 11, 5, 12, 4, 13, 3, 14, 2, 15, 1, 0]
AHEAD = 8


def kept(me):
    w = (me // NZ + NY - (me % NZ) // 4) % NY
    return w // 2, w % 2


def part(q_t, k, v, mask, before):
    s = jnp.dot(k, q_t, preferred_element_type=jnp.float32)
    if mask is not None:
        s = mask(s)
    m = jnp.max(s, axis=0, keepdims=True)
    if before is not None:
        m = jnp.maximum(m, before[0])
    p = jnp.exp2((s - m) * SCALE).astype(jnp.bfloat16)
    v_t = jnp.concatenate([v.T, jnp.ones((PIECE, v.shape[0]), v.dtype)], axis=0)
    total = jnp.dot(v_t, p, preferred_element_type=jnp.float32)
    if before is not None:
        total += before[1] * jnp.exp2((before[0] - m) * SCALE)
    return m, total


def kernel(
    queries, keys, values, selected, out,
    q_ref, q_t, sel, own, pieces, picked, fetched, top, acc,
    q_sem, sel_sem, head_send, head_recv, spread_send, spread_recv, fetch_send, fetch_recv,
):
    me = lax.axis_index("ctx")
    head = lax.axis_index("head")
    x, core = head // 2, head % 2

    barrier = pltpu.get_barrier_semaphore()

    y, z = me // NZ, me % NZ
    rows_y = [((y + j) % NY) * NZ for j in range(NY)]
    others = [(n, rows_y[j] + z_to) for n, z_to in enumerate((z + dz) % NZ for dz in STEPS) for j in (2, 1, 3, 0)][:-1]
    for _, to in others:
        pl.semaphore_signal(barrier, inc=1, device_id={"ctx": to}, device_id_type=MESH)
    for j in range(1, KVH):
        pl.semaphore_signal(barrier, inc=1, device_id={"head": (head + j) % KVH}, device_id_type=MESH)

    q_copy = pltpu.make_async_copy(queries, q_ref, q_sem)
    q_copy.start()
    sel_copy = pltpu.make_async_copy(selected, sel, sel_sem)
    sel_copy.start()
    for kv, source in enumerate((keys, values)):
        columns = pl.ds(pl.multiple_of(head * HD, HD), HD)
        pltpu.make_async_copy(source.at[:, columns], own.at[kv, head], head_recv.at[head]).start()
    sel_copy.wait()

    pl.semaphore_wait(barrier, NB - 1 + KVH - 1)

    order = [(dx, dk) for dx in (0, 1, 3, 2) for dk in (0, 1)]
    for dx, dk in order[1:]:
        g = ((x + dx) % 4) * 2 + (core + dk) % 2
        for kv, source in enumerate((keys, values)):
            columns = pl.ds(pl.multiple_of(g * HD, HD), HD)
            pltpu.make_async_remote_copy(
                src_ref=source.at[:, columns], dst_ref=own.at[kv, head], send_sem=head_send,
                recv_sem=head_recv.at[head], device_id={"head": g}, device_id_type=MESH,
            ).start()

    for dx, dk in order:
        g = ((x + (4 - dx)) % 4) * 2 + (core + dk) % 2
        pltpu.make_async_copy(own.at[:, g], own.at[:, g], head_recv.at[g]).wait()
        for off in (2, 1, 3, 0):
            j = (z // 4 + off) % 4
            for kv in range(2):
                to = ((2 * kv + g // 4 + j) % NY) * NZ + 4 * j + g % 4
                source = own.at[kv, g, pl.ds(pl.multiple_of(PIECE * j, PIECE), PIECE)]

                def remote(source=source, to=to):
                    pltpu.make_async_remote_copy(
                        src_ref=source, dst_ref=pieces.at[me], send_sem=spread_send,
                        recv_sem=spread_recv, device_id={"ctx": to}, device_id_type=MESH,
                    ).start()

                if off:
                    remote()
                else:
                    pl.when(to != me)(remote)

                    @pl.when(to == me)
                    def _():
                        pltpu.make_async_copy(source, pieces.at[me], spread_recv).start()

    pltpu.make_async_copy(pieces, pieces, spread_recv).wait()

    kv, half = kept(me)

    def pick(d):
        picked[d, 0] = pieces[sel[1, 0, d]]
        picked[d, 1] = pieces[sel[2, 0, d]]

    per_group = NZ // GROUPS
    for _, d in others[:AHEAD]:
        pick(d)
    for t, (n, d) in enumerate(others):
        pltpu.make_async_remote_copy(
            src_ref=picked.at[d], dst_ref=fetched.at[n, kv, half], send_sem=fetch_send,
            recv_sem=fetch_recv.at[n // per_group], device_id={"ctx": d}, device_id_type=MESH,
        ).start()
        if t + AHEAD < NB - 1:
            pick(others[t + AHEAD][1])
    last = NZ - 1
    pick(me)

    q_copy.wait()
    pltpu.make_async_copy(picked.at[me], fetched.at[last, kv, half], fetch_recv.at[GROUPS - 1]).start()
    for h in range(QH):
        q_t[:, h * BLK : (h + 1) * BLK] = q_ref[:, h * HD : (h + 1) * HD].T
    half_block = BLK // 2
    before = None
    for c in range(2):
        low = c * half_block

        def causal(s):
            key = lax.broadcasted_iota(jnp.int32, s.shape, 0) + low
            return jnp.where(key <= lax.broadcasted_iota(jnp.int32, s.shape, 1) % BLK, s, -jnp.inf)

        k = own[0].reshape(BLK, HD)[low : low + half_block]
        v = own[1].reshape(BLK, HD)[low : low + half_block]
        before = part(q_t[...], k, v, causal, before)
        top[...], acc[...] = before
        before = top[...], acc[...]

    gone = [jnp.where(sel[s + 1, 0, me] != me, 0.0, -jnp.inf).astype(jnp.float32) for s in range(2)]
    shape = (NB // NY // GROUPS * 4, PIECE, 1)
    slot = lax.broadcasted_iota(jnp.int32, shape, 0) % 2
    bias = jnp.where(slot == 0, gone[0], gone[1]).reshape(shape[0] * PIECE, 1)
    for g in range(GROUPS):
        planes = slice(g * (NZ // GROUPS), (g + 1) * (NZ // GROUPS))
        pltpu.make_async_copy(fetched.at[planes], fetched.at[planes], fetch_recv.at[g]).wait()
        k = fetched[planes, 0].reshape(-1, HD)
        v = fetched[planes, 1].reshape(-1, HD)
        before = part(q_t[...], k, v, lambda s: s + bias, (top[...], acc[...]))
        if g < GROUPS - 1:
            top[...], acc[...] = before
    total = before[1]
    for h in range(QH):
        t = total[:, h * BLK : (h + 1) * BLK]
        columns = slice(h * HD, (h + 1) * HD)
        out[:, columns] = (t[:HD] / t[HD : HD + 1]).astype(out.dtype).T

    most = pl.ds(0, KVH - 1)
    pltpu.make_async_copy(own.at[:, most], own.at[:, most], head_send).wait()
    most = pl.ds(0, NB - 1)
    pltpu.make_async_copy(pieces.at[most], pieces.at[most], spread_send).wait()
    pltpu.make_async_copy(picked.at[most], picked.at[most], fetch_send).wait()


def on_device(queries, keys, values, selected):
    dma = pltpu.SemaphoreType.DMA
    hbm = pl.BlockSpec(memory_space=pl.ANY)
    return pl.pallas_call(
        kernel,
        out_shape=pltpu.VMEM((BLK, QH * HD), jnp.bfloat16),
        in_specs=[hbm, hbm, hbm, hbm],
        out_specs=pl.BlockSpec(memory_space=pltpu.VMEM),
        scratch_shapes=[
            pltpu.VMEM((BLK, QH * HD), jnp.bfloat16),
            pltpu.VMEM((HD, QH * BLK), jnp.bfloat16),
            pltpu.SMEM((3, 1, NB), jnp.int32),
            pltpu.VMEM((2, KVH, SLICE, HD), jnp.bfloat16),
            pltpu.VMEM((NB, PIECE, HD), jnp.bfloat16),
            pltpu.VMEM((NB, 2, PIECE, HD), jnp.bfloat16),
            pltpu.VMEM((NZ, 2, 2, 2, PIECE, HD), jnp.bfloat16),
            pltpu.VMEM((1, QH * BLK), jnp.float32),
            pltpu.VMEM((HD + PIECE, QH * BLK), jnp.float32),
            dma, dma, dma, dma((KVH,)), dma, dma, dma, dma((GROUPS,)),
        ],
        compiler_params=pltpu.CompilerParams(collective_id=0, has_side_effects=True),
    )(queries, keys, values, selected.transpose(2, 0, 1))


def solution(mesh):
    return jax.shard_map(
        on_device,
        mesh=mesh,
        in_specs=(
            P("ctx", "head"),
            P(("ctx", "head"), None),
            P(("ctx", "head"), None),
            P("head", None, None),
        ),
        out_specs=P("ctx", "head"),
        check_vma=False,
    )
```

time: 73.5 us -> 60.9 us (0.83); the launches traced: 72.2 us -> 60.7 us
  Pallas kernels: 68.9 us -> 59.9 us
  local copies, waits for them, and re-layouts: 3.25 us -> 0.8 us
    pallas_call x1, Pallas kernels: 68.9 us -> 59.9 us  [on_device(): pl.pallas_call(kernel, out_shape=pltpu.VMEM((BLK, QH * HD), jnp.bfloat16)...]
    unnamed x2 -> x1, local copies, waits for them, and re-layouts: 3.25 us -> 0.8 us
where the time goes in v2:
time: 60.9 us; the launch traced here: 60.7 us
  Pallas kernels  59.9 us (98%)
  local copies, waits for them, and re-layouts  0.8 us (1%)
    pallas_call x1, Pallas kernels, on_device(): pl.pallas_call(kernel, out_shape=pltpu.VMEM((BLK, QH * HD), jnp.bfloat16)...  59.9 us

profile of v2, /device:TPU:24, one launch (start us, length us, event | category | flops | bytes accessed | tf_op | source)
XLA Modules:
  0.0 60.7 jit_solution(12840508657781036866)
XLA Ops:
  0.0 59.9 %shard_map.46 = bf16[512,512]{1,0:T(8,128)(2,1)S(1)} custom-call(bf16[512,512]{1,0:T(8,128)(2,1)} %queries.1, bf16[64,1024]{1,0:T(8,128)(2,1)} %keys.1, bf16[64,1024]{1,0:T(8,128)(2,1)} %values.1, s32[3,1,64]{2,1,0:T(1,128)} %bitcast.1), custom_call_target="tpu_custom_call" | custom-call | tf_op jit(solution)/shard_map/pallas_call | solution.py:182
  60.0 0.8 %copy.6 = bf16[512,512]{1,0:T(8,128)(2,1)} copy(bf16[512,512]{1,0:T(8,128)(2,1)S(1)} %shard_map.46) | data formatting | bytes 1048576

commit v3 on v2

--- a/solution.py
+++ b/solution.py
@@ -60,7 +60,7 @@
 
     y, z = me // NZ, me % NZ
     rows_y = [((y + j) % NY) * NZ for j in range(NY)]
-    others = [(n, rows_y[j] + z_to) for n, z_to in enumerate((z + dz) % NZ for dz in STEPS) for j in (2, 1, 3, 0)][:-1]
+    others = [(n, rows_y[j] + z_to) for n, z_to in enumerate((z + dz + core * (NZ - 2 * dz) + NZ) % NZ for dz in STEPS) for j in (2, 1, 3, 0)][:-1]
     for _, to in others:
         pl.semaphore_signal(barrier, inc=1, device_id={"ctx": to}, device_id_type=MESH)
     for j in range(1, KVH):
@@ -111,6 +111,24 @@
                     def _():
                         pltpu.make_async_copy(source, pieces.at[me], spread_recv).start()
 
+    q_copy.wait()
+    for h in range(QH):
+        q_t[:, h * BLK : (h + 1) * BLK] = q_ref[:, h * HD : (h + 1) * HD].T
+    half_block = BLK // 2
+    before = None
+    for c in range(2):
+        low = c * half_block
+
+        def causal(s):
+            key = lax.broadcasted_iota(jnp.int32, s.shape, 0) + low
+            return jnp.where(key <= lax.broadcasted_iota(jnp.int32, s.shape, 1) % BLK, s, -jnp.inf)
+
+        k = own[0].reshape(BLK, HD)[low : low + half_block]
+        v = own[1].reshape(BLK, HD)[low : low + half_block]
+        before = part(q_t[...], k, v, causal, before)
+        top[...], acc[...] = before
+        before = top[...], acc[...]
+
     pltpu.make_async_copy(pieces, pieces, spread_recv).wait()
 
     kv, half = kept(me)
@@ -120,6 +138,7 @@
         picked[d, 1] = pieces[sel[2, 0, d]]
 
     per_group = NZ // GROUPS
+    pick(me)
     for _, d in others[:AHEAD]:
         pick(d)
     for t, (n, d) in enumerate(others):
@@ -130,27 +149,8 @@
         if t + AHEAD < NB - 1:
             pick(others[t + AHEAD][1])
     last = NZ - 1
-    pick(me)
-
-    q_copy.wait()
+
     pltpu.make_async_copy(picked.at[me], fetched.at[last, kv, half], fetch_recv.at[GROUPS - 1]).start()
-    for h in range(QH):
-        q_t[:, h * BLK : (h + 1) * BLK] = q_ref[:, h * HD : (h + 1) * HD].T
-    half_block = BLK // 2
-    before = None
-    for c in range(2):
-        low = c * half_block
-
-        def causal(s):
-            key = lax.broadcasted_iota(jnp.int32, s.shape, 0) + low
-            return jnp.where(key <= lax.broadcasted_iota(jnp.int32, s.shape, 1) % BLK, s, -jnp.inf)
-
-        k = own[0].reshape(BLK, HD)[low : low + half_block]
-        v = own[1].reshape(BLK, HD)[low : low + half_block]
-        before = part(q_t[...], k, v, causal, before)
-        top[...], acc[...] = before
-        before = top[...], acc[...]
-
     gone = [jnp.where(sel[s + 1, 0, me] != me, 0.0, -jnp.inf).astype(jnp.float32) for s in range(2)]
     shape = (NB // NY // GROUPS * 4, PIECE, 1)
     slot = lax.broadcasted_iota(jnp.int32, shape, 0) % 2

time: 60.9 us -> 60.7 us (level)
    pallas_call x1, Pallas kernels: 59.9 us -> 59.3 us  [on_device(): pl.pallas_call(kernel, out_shape=pltpu.VMEM((BLK, QH * HD), jnp.bfloat16)...]
where the time goes in v3:
time: 60.7 us; the launch traced here: 60.1 us
  Pallas kernels  59.3 us (98%)
  local copies, waits for them, and re-layouts  0.8 us (1%)
    pallas_call x1, Pallas kernels, on_device(): pl.pallas_call(kernel, out_shape=pltpu.VMEM((BLK, QH * HD), jnp.bfloat16)...  59.3 us

profile of v3, /device:TPU:24, one launch (start us, length us, event | category | flops | bytes accessed | tf_op | source)
XLA Modules:
  0.0 60.1 jit_solution(2256284443005701506)
XLA Ops:
  0.0 59.3 %shard_map.46 = bf16[512,512]{1,0:T(8,128)(2,1)S(1)} custom-call(bf16[512,512]{1,0:T(8,128)(2,1)} %queries.1, bf16[64,1024]{1,0:T(8,128)(2,1)} %keys.1, bf16[64,1024]{1,0:T(8,128)(2,1)} %values.1, s32[3,1,64]{2,1,0:T(1,128)} %bitcast.1), custom_call_target="tpu_custom_call" | custom-call | tf_op jit(solution)/shard_map/pallas_call | solution.py:182
  59.3 0.8 %copy.6 = bf16[512,512]{1,0:T(8,128)(2,1)} copy(bf16[512,512]{1,0:T(8,128)(2,1)S(1)} %shard_map.46) | data formatting | bytes 1048576

commit v4 on v3

--- a/solution.py
+++ b/solution.py
@@ -77,7 +77,7 @@
 
     pl.semaphore_wait(barrier, NB - 1 + KVH - 1)
 
-    order = [(dx, dk) for dx in (0, 1, 3, 2) for dk in (0, 1)]
+    order = [(0, 0), (0, 1), (1, 0), (3, 0), (1, 1), (3, 1), (2, 0), (2, 1)]
     for dx, dk in order[1:]:
         g = ((x + dx) % 4) * 2 + (core + dk) % 2
         for kv, source in enumerate((keys, values)):

time: 60.7 us -> 60.3 us (level)
  no operation moved by 1% of the time
where the time goes in v4:
time: 60.3 us; the launch traced here: 59.8 us
  Pallas kernels  59 us (98%)
  local copies, waits for them, and re-layouts  0.8 us (1%)
    pallas_call x1, Pallas kernels, on_device(): pl.pallas_call(kernel, out_shape=pltpu.VMEM((BLK, QH * HD), jnp.bfloat16)...  59 us

profile of v4, /device:TPU:24, one launch (start us, length us, event | category | flops | bytes accessed | tf_op | source)
XLA Modules:
  0.0 59.8 jit_solution(13835907623797723055)
XLA Ops:
  0.0 59.0 %shard_map.46 = bf16[512,512]{1,0:T(8,128)(2,1)S(1)} custom-call(bf16[512,512]{1,0:T(8,128)(2,1)} %queries.1, bf16[64,1024]{1,0:T(8,128)(2,1)} %keys.1, bf16[64,1024]{1,0:T(8,128)(2,1)} %values.1, s32[3,1,64]{2,1,0:T(1,128)} %bitcast.1), custom_call_target="tpu_custom_call" | custom-call | tf_op jit(solution)/shard_map/pallas_call | solution.py:182
  59.1 0.8 %copy.6 = bf16[512,512]{1,0:T(8,128)(2,1)} copy(bf16[512,512]{1,0:T(8,128)(2,1)S(1)} %shard_map.46) | data formatting | bytes 1048576

commit v5 on v3

--- a/solution.py
+++ b/solution.py
@@ -164,10 +164,11 @@
         if g < GROUPS - 1:
             top[...], acc[...] = before
     total = before[1]
+    share = 1.0 / total[HD : HD + 1]
     for h in range(QH):
-        t = total[:, h * BLK : (h + 1) * BLK]
+        t = slice(h * BLK, (h + 1) * BLK)
         columns = slice(h * HD, (h + 1) * HD)
-        out[:, columns] = (t[:HD] / t[HD : HD + 1]).astype(out.dtype).T
+        out[:, columns] = (total[:HD, t] * share[:, t]).astype(out.dtype).T
 
     most = pl.ds(0, KVH - 1)
     pltpu.make_async_copy(own.at[:, most], own.at[:, most], head_send).wait()

time: 60.7 us -> 60.7 us (level)
  no operation moved by 1% of the time
where the time goes in v5:
time: 60.7 us; the launch traced here: 60.1 us
  Pallas kernels  59.2 us (98%)
  local copies, waits for them, and re-layouts  0.8 us (1%)
    pallas_call x1, Pallas kernels, on_device(): pl.pallas_call(kernel, out_shape=pltpu.VMEM((BLK, QH * HD), jnp.bfloat16)...  59.2 us

profile of v5, /device:TPU:24, one launch (start us, length us, event | category | flops | bytes accessed | tf_op | source)
XLA Modules:
  0.0 60.1 jit_solution(5797150732649841171)
XLA Ops:
  0.0 59.2 %shard_map.46 = bf16[512,512]{1,0:T(8,128)(2,1)S(1)} custom-call(bf16[512,512]{1,0:T(8,128)(2,1)} %queries.1, bf16[64,1024]{1,0:T(8,128)(2,1)} %keys.1, bf16[64,1024]{1,0:T(8,128)(2,1)} %values.1, s32[3,1,64]{2,1,0:T(1,128)} %bitcast.1), custom_call_target="tpu_custom_call" | custom-call | tf_op jit(solution)/shard_map/pallas_call | solution.py:183
  59.3 0.8 %copy.6 = bf16[512,512]{1,0:T(8,128)(2,1)} copy(bf16[512,512]{1,0:T(8,128)(2,1)S(1)} %shard_map.46) | data formatting | bytes 1048576
